TPU v7x, 32 devices: a whole 2x2x4 slice. The times are simulated.
32 devices in a mesh: lag: 4 (over y, x), row: 8 (over z, core).
Axes of the slice: x: 2, y: 2, z: 4, core: 2. Of those that a mesh axis runs over, the one named last changes fastest.
Arguments:
- lag_weights: float32 [16, 4096, 4096], P('lag', 'row'), may hold values from -0.0234375 to 0.0234375
- inverse_head: float32 [4096, 4096], P('row'), may hold values from -0.09375 to 0.09375
- excitation: float32 [3, 4096, 128], P(None, 'row'), may hold values from -6 to 6
- history: float32 [16, 4096, 128], P('lag', 'row'), may hold values from -6 to 6
Outputs:
- densities: float32 [3, 4096, 128], P(None, 'row')
All inputs are finite; a program needn't handle non-finite values.
Results may differ from a plain program's by a relative error of at most 0.0001.
Values sent between devices are 32-bit elements; how exact they have to be, the bound alone decides.
No kernel may reach another device: no remote copies, remote signals or barrier semaphores. Data moves between devices by JAX's collectives and lax.ppermute only.
A program may use at most 128 MiB of HBM per device.

v0:
```python
import jax
import jax.numpy as jnp
from jax import lax
from jax.sharding import PartitionSpec as P

STEPS = 3


def from_behind(value, axis, steps):
    count = lax.axis_size(axis)
    leading, last = (max(0, -steps), min(count, count - steps))
    return lax.ppermute(value, axis, [(source, source + steps) for source in range(leading, last)])


def lag_products(weights, piece):
    return jnp.einsum("kmc,kcr->mr", weights, piece, precision=lax.Precision.HIGHEST)


def on_device(lag_weights, inverse_head, excitation, history):
    at_head = lax.axis_index("lag") == 0
    past = lax.all_gather(history, "row", axis=1, tiled=True)
    results = []
    for step in range(STEPS):
        carried = lag_products(lag_weights, past)
        carried = lax.psum(carried, "lag")
        right_side = excitation[step] - carried
        density = jnp.dot(
            inverse_head,
            lax.all_gather(right_side, "row", axis=0, tiled=True),
            precision=lax.Precision.HIGHEST,
            preferred_element_type=jnp.float32,
        )
        results.append(density)
        if step + 1 < STEPS:
            whole_density = lax.all_gather(density, "row", axis=0, tiled=True)
            moved = from_behind(past[-1], "lag", 1)
            entering = jnp.where(at_head, whole_density, moved)
            past = jnp.concatenate([entering[None], past[:-1]], axis=0)
    return jnp.stack(results, axis=0)


def solution(mesh):
    placed = (P("lag", "row", None), P("row", None), P(None, "row", None), P("lag", "row", None))
    return jax.shard_map(
        on_device, mesh=mesh, in_specs=placed, out_specs=P(None, "row", None), check_vma=False
    )
```

profile of v0, /device:TPU:0, one launch (start us, length us, event | category | flops | bytes accessed | tf_op | source)
XLA Modules:
  0.0 563.5 jit_solution(13473457763976468164)
XLA Ops:
  6.5 0.0 all-gather.7.cloned.1.call-start
  6.5 2.6 copy.5
  9.2 0.0 all-gather.7.cloned.1.call-update
  9.2 0.0 copy-start.4
  9.2 0.0 all-reduce.4.cloned.1.call-start
  9.3 84.8 %all-gather.7.cloned.1.call-done = f32[4,4096,128]{1,2,0:T(8,128)} async-done(((f32[4,512,128]{1,2,0:T(8,128)}), f32[4,4096,128]{1,2,0:T(8,128)}) %all-gather.7.cloned.1.call-update) | async-done | bytes 8388624 | tf_op jit(solution)/shard_map/all_gather | solution.py:21
  94.1 31.3 %convolution_bitcast_fusion.1 = f32[512,128]{1,0:T(8,128)} fusion(f32[4,512,4096]{2,1,0:T(8,128)} %param.4, f32[4,4096,128]{1,2,0:T(8,128)} %all-gather.7.cloned.1.call-done), kind=kOutput, calls=%fused_computation.16 | convolution fusion | flops 12884901888 | bytes 42205184 | tf_op jit(solution)/shard_map/kmc,kcr->mr/dot_general | solution.py:16
  125.4 0.0 all-reduce.4.cloned.1.call-update
  125.5 0.0 all-gather.9.cloned.1.call-start
  125.5 41.6 %all-reduce.4.cloned.1.call-done = f32[512,128]{1,0:T(8,128)} async-done(((f32[512,128]{1,0:T(8,128)}), f32[512,128]{1,0:T(8,128)}) %all-reduce.4.cloned.1.call-update) | async-done | bytes 262160 | tf_op jit(solution)/shard_map/psum | solution.py:25
  167.1 1.7 bitcast_subtract_fusion.2
  168.8 0.0 all-gather.9.cloned.1.call-update
  168.8 0.3 all-gather.11.cloned.1.call-start
  169.2 29.0 %all-gather.9.cloned.1.call-done = f32[4096,128]{1,0:T(8,128)} async-done(((f32[512,128]{1,0:T(8,128)}), f32[4096,128]{1,0:T(8,128)}) %all-gather.9.cloned.1.call-update) | async-done | bytes 2097168 | tf_op jit(solution)/shard_map/all_gather | solution.py:29
  198.1 13.5 %fusion.17 = f32[128,512]{1,0:T(8,128)} fusion(f32[4096,128]{1,0:T(8,128)} %all-gather.9.cloned.1.call-done, f32[512,4096]{1,0:T(8,128)} %param.5), kind=kOutput, calls=%fused_computation.23 | convolution fusion | flops 3221225472 | bytes 10747904 | tf_op jit(solution)/shard_map/dot_general | solution.py:27
  211.7 0.0 all-gather.11.cloned.1.call-update
  211.7 0.0 all-reduce.6.cloned.1.call-start
  211.7 4.7 slice_bitcast_fusion
  216.4 4.0 collective-permute-start
  220.4 6.2 %slice.30 = f32[3,4096,128]{1,2,0:T(8,128)} slice(f32[4,4096,128]{1,2,0:T(8,128)} %all-gather.7.cloned.1.call-done), slice={[0:3], [0:4096], [0:128]} | slice | bytes 12582912 | tf_op jit(solution)/shard_map/slice | solution.py:38
  226.6 38.7 %collective-permute-done = f32[4096,128]{0,1:T(8,128)S(1)} collective-permute-done((f32[4096,128]{0,1:T(8,128)}, f32[4096,128]{0,1:T(8,128)S(1)}, u32[]{:S(2)}, u32[]{:S(2)}) %collective-permute-start) | collective-permute-done | bytes 2097184 | tf_op jit(solution)/shard_map/ppermute | solution.py:12
  265.3 1.3 copy-done.3
  266.7 2.0 select_bitcast_fusion.1
  268.6 1.4 copy-done
  270.1 30.9 %fusion.12 = f32[512,128]{1,0:T(8,128)} fusion(f32[4,512,4096]{2,1,0:T(8,128)} %param.4, f32[3,4096,128]{1,2,0:T(8,128)S(1)} %copy-done, f32[1,4096,128]{1,2,0:T(8,128)S(1)} %select_bitcast_fusion.1), kind=kOutput, calls=%fused_computation.15 | convolution fusion | flops 12886999040 | bytes 42205184 | tf_op jit(solution)/shard_map/kmc,kcr->mr/dot_general | solution.py:16
  301.0 0.0 all-reduce.6.cloned.1.call-update
  301.0 0.0 all-gather.13.cloned.1.call-start
  301.0 43.5 %all-reduce.6.cloned.1.call-done = f32[512,128]{1,0:T(8,128)} async-done(((f32[512,128]{1,0:T(8,128)}), f32[512,128]{1,0:T(8,128)}) %all-reduce.6.cloned.1.call-update) | async-done | bytes 262160 | tf_op jit(solution)/shard_map/psum | solution.py:25
  344.5 1.7 bitcast_subtract_fusion.1
  346.2 0.0 all-gather.13.cloned.1.call-update
  346.2 0.2 all-gather.15.cloned.1.call-start
  346.4 29.1 %all-gather.13.cloned.1.call-done = f32[4096,128]{1,0:T(8,128)} async-done(((f32[512,128]{1,0:T(8,128)}), f32[4096,128]{1,0:T(8,128)}) %all-gather.13.cloned.1.call-update) | async-done | bytes 2097168 | tf_op jit(solution)/shard_map/all_gather | solution.py:29
  375.5 13.5 %fusion.18 = f32[128,512]{1,0:T(8,128)} fusion(f32[4096,128]{1,0:T(8,128)} %all-gather.13.cloned.1.call-done, f32[512,4096]{1,0:T(8,128)} %param.5), kind=kOutput, calls=%fused_computation.24 | convolution fusion | flops 3221225472 | bytes 10747904 | tf_op jit(solution)/shard_map/dot_general | solution.py:27
  389.0 0.0 all-gather.15.cloned.1.call-update
  389.1 0.0 all-reduce.8.cloned.1.call-start
  389.1 4.9 collective-permute-start.1
  394.0 44.1 %collective-permute-done.1 = f32[4096,128]{0,1:T(8,128)} collective-permute-done((f32[4096,128]{0,1:T(8,128)}, f32[4096,128]{0,1:T(8,128)}, u32[]{:S(2)}, u32[]{:S(2)}) %collective-permute-start.1) | collective-permute-done | bytes 2097184 | tf_op jit(solution)/shard_map/ppermute | solution.py:12
  438.1 1.8 select_bitcast_fusion
  439.9 31.1 %fusion.9 = f32[512,128]{1,0:T(8,128)} fusion(f32[4,512,4096]{2,1,0:T(8,128)} %param.4, f32[3,4096,128]{1,2,0:T(8,128)} %slice.30, f32[1,4096,128]{1,2,0:T(8,128)S(1)} %select_bitcast_fusion.1, f32[1,4096,128]{1,2,0:T(8,128)S(1)} %select_bitcast_fusion), kind=kOutput, calls=%fused_computation.13 | convolution fusion | flops 12889096192 | bytes 44302336 | tf_op jit(solution)/shard_map/kmc,kcr->mr/dot_general | solution.py:16
  471.0 0.0 all-reduce.8.cloned.1.call-update
  471.0 0.0 all-gather.17.cloned.1.call-start
  471.1 43.6 %all-reduce.8.cloned.1.call-done = f32[512,128]{1,0:T(8,128)} async-done(((f32[512,128]{1,0:T(8,128)}), f32[512,128]{1,0:T(8,128)}) %all-reduce.8.cloned.1.call-update) | async-done | bytes 262160 | tf_op jit(solution)/shard_map/psum | solution.py:25
  514.6 1.7 bitcast_subtract_fusion
  516.3 0.0 all-gather.17.cloned.1.call-update
  516.4 29.3 %all-gather.17.cloned.1.call-done = f32[4096,128]{1,0:T(8,128)} async-done(((f32[512,128]{1,0:T(8,128)}), f32[4096,128]{1,0:T(8,128)}) %all-gather.17.cloned.1.call-update) | async-done | bytes 2097168 | tf_op jit(solution)/shard_map/all_gather | solution.py:29
  545.7 9.9 %convolution_bitcast_fusion = f32[1,512,128]{1,2,0:T(8,128)S(1)} fusion(f32[4096,128]{1,0:T(8,128)} %all-gather.17.cloned.1.call-done, f32[512,4096]{1,0:T(8,128)} %param.5), kind=kOutput, calls=%fused_computation.14 | convolution fusion | flops 3221225472 | bytes 10747904 | tf_op jit(solution)/shard_map/dot_general | solution.py:27
  555.6 0.1 pad_maximum_fusion.1
  555.6 1.1 copy.6
  (9 shorter events, 0.0 us)
Async XLA Ops:
  6.5 87.6 %all-gather.7.cloned.1.call-start = ((), (), s32[]{:S(2)}) async-start(), calls=%async_computation | async-start | bytes 9437184 | tf_op jit(solution)/shard_map/all_gather | solution.py:21
  9.2 157.9 %copy-start.4 = (f32[3,512,128]{2,1,0:T(8,128)S(1)}, f32[3,512,128]{2,1,0:T(8,128)}, u32[]{:S(2)}) copy-start(f32[3,512,128]{2,1,0:T(8,128)} %param.6) | copy-start | bytes 2359300
  9.2 157.9 %all-reduce.4.cloned.1.call-start = ((), (), s32[]{:S(2)}) async-start(), calls=%async_computation.1 | async-start | bytes 524288 | tf_op jit(solution)/shard_map/psum | solution.py:25
  125.5 72.7 %all-gather.9.cloned.1.call-start = ((), (), s32[]{:S(2)}) async-start(), calls=%async_computation.2 | async-start | bytes 2359296 | tf_op jit(solution)/shard_map/all_gather | solution.py:29
  168.8 97.8 %all-gather.11.cloned.1.call-start = ((), (), s32[]{:S(2)}) async-start(), calls=%async_computation.3 | async-start | bytes 2359296 | tf_op jit(solution)/shard_map/all_gather | solution.py:35
  211.7 132.8 %all-reduce.6.cloned.1.call-start = ((), (), s32[]{:S(2)}) async-start(), calls=%async_computation.4 | async-start | bytes 524288 | tf_op jit(solution)/shard_map/psum | solution.py:25
  216.4 48.9 %collective-permute-start = (f32[4096,128]{0,1:T(8,128)}, f32[4096,128]{0,1:T(8,128)S(1)}, u32[]{:S(2)}, u32[]{:S(2)}) collective-permute-start(f32[4096,128]{0,1:T(8,128)} %get-tuple-element.6), channel_id=1, source_target_pairs={{0,8},{8,16},{16,24},{1,9},{9,17},{17,25},{2,10},{10,18},{18,26},{... | collective-permute-start | bytes 6291464 | tf_op jit(solution)/shard_map/ppermute | solution.py:12
  265.3 1.3 copy-start.3
  266.7 3.4 copy-start
  301.0 74.5 %all-gather.13.cloned.1.call-start = ((), (), s32[]{:S(2)}) async-start(), calls=%async_computation.5 | async-start | bytes 2359296 | tf_op jit(solution)/shard_map/all_gather | solution.py:29
  346.2 91.9 %all-gather.15.cloned.1.call-start = ((), (), s32[]{:S(2)}) async-start(), calls=%async_computation.6 | async-start | bytes 2359296 | tf_op jit(solution)/shard_map/all_gather | solution.py:35
  389.1 125.6 %all-reduce.8.cloned.1.call-start = ((), (), s32[]{:S(2)}) async-start(), calls=%async_computation.7 | async-start | bytes 524288 | tf_op jit(solution)/shard_map/psum | solution.py:25
  389.1 49.0 %collective-permute-start.1 = (f32[4096,128]{0,1:T(8,128)}, f32[4096,128]{0,1:T(8,128)}, u32[]{:S(2)}, u32[]{:S(2)}) collective-permute-start(f32[4096,128]{0,1:T(8,128)} %get-tuple-element.5), channel_id=1, source_target_pairs={{0,8},{8,16},{16,24},{1,9},{9,17},{17,25},{2,10},{10,18},{18,26},{... | collective-permute-start | bytes 6291464 | tf_op jit(solution)/shard_map/ppermute | solution.py:12
  471.0 84.5 %copy-start.1 = (f32[128,512]{1,0:T(8,128)S(1)}, f32[128,512]{1,0:T(8,128)}, u32[]{:S(2)}) copy-start(f32[128,512]{1,0:T(8,128)} %fusion.17) | copy-start | bytes 786436
  471.0 84.5 %copy-start.2 = (f32[128,512]{1,0:T(8,128)S(1)}, f32[128,512]{1,0:T(8,128)}, u32[]{:S(2)}) copy-start(f32[128,512]{1,0:T(8,128)} %fusion.18) | copy-start | bytes 786436
  471.0 74.6 %all-gather.17.cloned.1.call-start = ((), (), s32[]{:S(2)}) async-start(), calls=%async_computation.8 | async-start | bytes 2359296 | tf_op jit(solution)/shard_map/all_gather | solution.py:29
Sparse Core Ops, SparseCore 0:
  9.3 84.7 all-gather.6
  125.6 41.5 all-reduce.3
  169.0 29.1 all-gather.8
  211.8 28.5 all-gather.10
  301.1 43.3 all-reduce.5
  346.3 29.1 all-gather.12
  389.2 28.5 all-gather.14
  471.2 43.4 all-reduce.7
  516.5 29.1 all-gather.16
where the time goes:
time: 570 us; the launch traced here: 564 us
  waiting for transfers between devices  384 us (67%)
  matrix products  130 us (23%)
  local copies, waits for them, and re-layouts  17.4 us (3%)
  between operations  13.5 us (2%)
  starting transfers between devices  9.68 us (2%)
  other arithmetic  8.88 us (2%)
    psum x3, waiting for transfers between devices, on_device(): carried = lax.psum(carried, 'lag')  129 us
    dot_general x3, matrix products, lag_products(): jnp.einsum('kmc,kcr->mr', weights, piece, precision=lax.Precision.HIGHEST)  93.3 us
    all_gather x3, waiting for transfers between devices, on_device(): lax.all_gather(right_side, 'row', axis=0, tiled=True)  87.4 us
    all_gather x1, waiting for transfers between devices, on_device(): past = lax.all_gather(history, 'row', axis=1, tiled=True)  84.8 us
    ppermute x2, waiting for transfers between devices, from_behind(): lax.ppermute(value, axis, [(source, source + steps) for source in range(l...  82.8 us
    dot_general x3, matrix products, on_device(): jnp.dot(inverse_head, lax.all_gather(right_side, 'row', axis=0, tiled=Tru...  36.9 us
  transfers between devices with their start and end apart: 11, of which 9 were waited for; matrix products, arithmetic and copies ran while one was open for 2% of the time, Pallas kernels for 0%

commit v1 on v0

--- a/solution.py
+++ b/solution.py
@@ -22,7 +22,8 @@
     results = []
     for step in range(STEPS):
         carried = lag_products(lag_weights, past)
-        carried = lax.psum(carried, "lag")
+        pieces = lax.all_gather(carried, "lag")
+        carried = jnp.sum(pieces, axis=0)
         right_side = excitation[step] - carried
         density = jnp.dot(
             inverse_head,

time: 570 us -> 529 us (0.928); the launches traced: 564 us -> 529 us
  waiting for transfers between devices: 384 us -> 336 us
  matrix products: 130 us -> 142 us
    psum x3 -> x0, waiting for transfers between devices: 129 us -> none  [on_device(): carried = lax.psum(carried, 'lag')]
    all_gather x0 -> x3, waiting for transfers between devices: none -> 77 us  [on_device(): pieces = lax.all_gather(carried, 'lag')]
    dot_general x3, matrix products: 93.3 us -> 112 us  [lag_products(): jnp.einsum('kmc,kcr->mr', weights, piece, precision=lax.Precision.HIGHEST)]
    dot_general x3, matrix products: 36.9 us -> 29.5 us  [on_device(): jnp.dot(inverse_head, lax.all_gather(right_side, 'row', axis=0, tiled=Tru...]
where the time goes in v1:
time: 529 us
  waiting for transfers between devices  336 us (64%)
  matrix products  142 us (27%)
  local copies, waits for them, and re-layouts  18.8 us (4%)
  between operations  13.3 us (3%)
  other arithmetic  10.4 us (2%)
  starting transfers between devices  8.95 us (2%)
    dot_general x3, matrix products, lag_products(): jnp.einsum('kmc,kcr->mr', weights, piece, precision=lax.Precision.HIGHEST)  112 us
    all_gather x3, waiting for transfers between devices, on_device(): lax.all_gather(right_side, 'row', axis=0, tiled=True)  87.8 us
    all_gather x1, waiting for transfers between devices, on_device(): past = lax.all_gather(history, 'row', axis=1, tiled=True)  86.4 us
    ppermute x2, waiting for transfers between devices, from_behind(): lax.ppermute(value, axis, [(source, source + steps) for source in range(l...  83.6 us
    all_gather x3, waiting for transfers between devices, on_device(): pieces = lax.all_gather(carried, 'lag')  77 us
    dot_general x3, matrix products, on_device(): jnp.dot(inverse_head, lax.all_gather(right_side, 'row', axis=0, tiled=Tru...  29.5 us
  transfers between devices with their start and end apart: 11, of which 9 were waited for; matrix products, arithmetic and copies ran while one was open for 2% of the time, Pallas kernels for 0%

profile of v1, /device:TPU:0, one launch (start us, length us, event | category | flops | bytes accessed | tf_op | source)
XLA Modules:
  0.0 528.9 jit_solution(16187300830743242943)
XLA Ops:
  6.5 0.7 all-gather.13.cloned.1.call-update
  7.3 0.0 all-gather.25.cloned.1.call-start
  7.3 86.4 %all-gather.13.cloned.1.call-done = f32[4,4096,128]{2,1,0:T(8,128)} async-done(((f32[4,512,128]{2,1,0:T(8,128)}), f32[4,4096,128]{2,1,0:T(8,128)}) %all-gather.13.cloned.1.call-update) | async-done | bytes 8388624 | tf_op jit(solution)/shard_map/all_gather | solution.py:21
  93.7 31.7 %convolution_bitcast_fusion.1 = f32[512,128]{1,0:T(8,128)} fusion(f32[4,512,4096]{2,1,0:T(8,128)} %param.4, f32[4,4096,128]{2,1,0:T(8,128)} %all-gather.13.cloned.1.call-done), kind=kOutput, calls=%fused_computation.16 | convolution fusion | flops 12884901888 | bytes 42205184 | tf_op jit(solution)/shard_map/kmc,kcr->mr/dot_general | solution.py:16
  125.4 0.0 all-gather.25.cloned.1.call-update
  125.4 0.0 all-gather.15.cloned.1.call-start
  125.5 25.1 %all-gather.25.cloned.1.call-done = f32[2048,128]{1,0:T(8,128)} async-done(((f32[512,128]{1,0:T(8,128)}), f32[2048,128]{1,0:T(8,128)}) %all-gather.25.cloned.1.call-update) | async-done | bytes 1048592 | tf_op jit(solution)/shard_map/all_gather | solution.py:25
  150.6 1.3 reduce_sum.27
  151.9 0.7 bitcast_subtract_fusion.2
  152.6 0.0 all-gather.15.cloned.1.call-update
  152.7 0.0 all-gather.17.cloned.1.call-start
  152.7 29.3 %all-gather.15.cloned.1.call-done = f32[4096,128]{1,0:T(8,128)} async-done(((f32[512,128]{1,0:T(8,128)}), f32[4096,128]{1,0:T(8,128)}) %all-gather.15.cloned.1.call-update) | async-done | bytes 2097168 | tf_op jit(solution)/shard_map/all_gather | solution.py:30
  182.0 10.1 %fusion.18 = f32[128,512]{0,1:T(8,128)} fusion(f32[4096,128]{1,0:T(8,128)} %all-gather.15.cloned.1.call-done, f32[512,4096]{1,0:T(8,128)} %param.5), kind=kOutput, calls=%fused_computation.24 | convolution fusion | flops 3221225472 | bytes 10747904 | tf_op jit(solution)/shard_map/dot_general | solution.py:28
  192.0 0.0 all-gather.17.cloned.1.call-update
  192.0 0.0 all-gather.27.cloned.1.call-start
  192.1 4.5 slice_bitcast_fusion
  196.6 3.7 collective-permute-start
  200.3 5.9 %slice.30 = f32[3,4096,128]{2,1,0:T(8,128)} slice(f32[4,4096,128]{2,1,0:T(8,128)} %all-gather.13.cloned.1.call-done), slice={[0:3], [0:4096], [0:128]} | slice | bytes 12582912 | tf_op jit(solution)/shard_map/slice | solution.py:39
  206.2 39.4 %collective-permute-done = f32[4096,128]{1,0:T(8,128)S(1)} collective-permute-done((f32[4096,128]{1,0:T(8,128)}, f32[4096,128]{1,0:T(8,128)S(1)}, u32[]{:S(2)}, u32[]{:S(2)}) %collective-permute-start) | collective-permute-done | bytes 2097184 | tf_op jit(solution)/shard_map/ppermute | solution.py:12
  245.5 1.3 copy-done.3
  246.9 2.0 select_bitcast_fusion.1
  248.9 1.4 copy-done
  250.3 40.6 %fusion.12 = f32[512,128]{0,1:T(8,128)} fusion(f32[4,512,4096]{2,1,0:T(8,128)} %param.4, f32[3,4096,128]{2,1,0:T(8,128)S(1)} %copy-done, f32[1,4096,128]{2,1,0:T(8,128)S(1)} %select_bitcast_fusion.1), kind=kOutput, calls=%fused_computation.15 | convolution fusion | flops 12886999040 | bytes 42205184 | tf_op jit(solution)/shard_map/kmc,kcr->mr/dot_general | solution.py:16
  290.9 0.0 all-gather.19.cloned.1.call-start
  291.0 0.7 fusion.17
  291.7 0.8 copy.22
  292.6 25.3 %all-gather.27.cloned.1.call-done = f32[2048,128]{0,1:T(8,128)} async-done(((f32[512,128]{0,1:T(8,128)}), f32[2048,128]{0,1:T(8,128)}) %all-gather.27.cloned.1.call-update) | async-done | bytes 1048592 | tf_op jit(solution)/shard_map/all_gather | solution.py:25
  317.9 1.9 reshape.1
  319.8 0.6 reduce_sum.28
  320.4 1.7 bitcast_subtract_fusion.1
  322.1 0.0 all-gather.19.cloned.1.call-update
  322.2 0.0 all-gather.21.cloned.1.call-start
  322.2 29.3 %all-gather.19.cloned.1.call-done = f32[4096,128]{0,1:T(8,128)} async-done(((f32[512,128]{0,1:T(8,128)}), f32[4096,128]{0,1:T(8,128)}) %all-gather.19.cloned.1.call-update) | async-done | bytes 2097168 | tf_op jit(solution)/shard_map/all_gather | solution.py:30
  351.5 10.1 %fusion.19 = f32[128,512]{0,1:T(8,128)} fusion(f32[4096,128]{0,1:T(8,128)} %all-gather.19.cloned.1.call-done, f32[512,4096]{1,0:T(8,128)} %param.5), kind=kOutput, calls=%fused_computation.25 | convolution fusion | flops 3221225472 | bytes 10747904 | tf_op jit(solution)/shard_map/dot_general | solution.py:28
  361.6 0.0 all-gather.29.cloned.1.call-start
  361.6 4.7 collective-permute-start.1
  366.3 44.3 %collective-permute-done.1 = f32[4096,128]{1,0:T(8,128)} collective-permute-done((f32[4096,128]{1,0:T(8,128)}, f32[4096,128]{1,0:T(8,128)}, u32[]{:S(2)}, u32[]{:S(2)}) %collective-permute-start.1) | collective-permute-done | bytes 2097184 | tf_op jit(solution)/shard_map/ppermute | solution.py:12
  410.6 1.8 select_bitcast_fusion
  412.4 39.9 %fusion.9 = f32[512,128]{0,1:T(8,128)} fusion(f32[4,512,4096]{2,1,0:T(8,128)} %param.4, f32[3,4096,128]{2,1,0:T(8,128)} %slice.30, f32[1,4096,128]{2,1,0:T(8,128)S(1)} %select_bitcast_fusion.1, f32[1,4096,128]{2,1,0:T(8,128)S(1)} %select_bitcast_fusion), kind=kOutput, calls=%fused_computation.13 | convolution fusion | flops 12889096192 | bytes 44302336 | tf_op jit(solution)/shard_map/kmc,kcr->mr/dot_general | solution.py:16
  452.3 0.3 all-gather.23.cloned.1.call-start
  452.7 0.1 copy.23
  452.8 26.6 %all-gather.29.cloned.1.call-done = f32[2048,128]{0,1:T(8,128)} async-done(((f32[512,128]{0,1:T(8,128)}), f32[2048,128]{0,1:T(8,128)}) %all-gather.29.cloned.1.call-update) | async-done | bytes 1048592 | tf_op jit(solution)/shard_map/all_gather | solution.py:25
  479.4 1.9 reshape.2
  481.4 0.6 reduce_sum.29
  482.0 0.7 bitcast_subtract_fusion
  482.7 29.3 %all-gather.23.cloned.1.call-done = f32[4096,128]{0,1:T(8,128)} async-done(((f32[512,128]{0,1:T(8,128)}), f32[4096,128]{0,1:T(8,128)}) %all-gather.23.cloned.1.call-update) | async-done | bytes 2097168 | tf_op jit(solution)/shard_map/all_gather | solution.py:30
  512.1 9.4 %convolution_bitcast_fusion = f32[1,512,128]{2,1,0:T(8,128)S(1)} fusion(f32[4096,128]{0,1:T(8,128)} %all-gather.23.cloned.1.call-done, f32[512,4096]{1,0:T(8,128)} %param.5), kind=kOutput, calls=%fused_computation.14 | convolution fusion | flops 3221225472 | bytes 10747904 | tf_op jit(solution)/shard_map/dot_general | solution.py:28
  521.5 0.9 pad_maximum_fusion.1
  (17 shorter events, 0.1 us)
Async XLA Ops:
  6.5 87.2 %all-gather.13.cloned.1.call-start = ((), (), s32[]{:S(2)}) async-start(), calls=%async_computation | async-start | bytes 9437184 | tf_op jit(solution)/shard_map/all_gather | solution.py:21
  7.3 144.6 %copy-start.5 = (f32[3,512,128]{2,1,0:T(8,128)S(1)}, f32[3,512,128]{2,1,0:T(8,128)}, u32[]{:S(2)}) copy-start(f32[3,512,128]{2,1,0:T(8,128)} %param.6) | copy-start | bytes 2359300
  7.3 143.3 %all-gather.25.cloned.1.call-start = ((), (), s32[]{:S(2)}) async-start(), calls=%async_computation.6 | async-start | bytes 1310720 | tf_op jit(solution)/shard_map/all_gather | solution.py:25
  125.4 56.5 %all-gather.15.cloned.1.call-start = ((), (), s32[]{:S(2)}) async-start(), calls=%async_computation.1 | async-start | bytes 2359296 | tf_op jit(solution)/shard_map/all_gather | solution.py:30
  152.7 94.2 %all-gather.17.cloned.1.call-start = ((), (), s32[]{:S(2)}) async-start(), calls=%async_computation.2 | async-start | bytes 2359296 | tf_op jit(solution)/shard_map/all_gather | solution.py:36
  192.0 125.8 %all-gather.27.cloned.1.call-start = ((), (), s32[]{:S(2)}) async-start(), calls=%async_computation.7 | async-start | bytes 1310720 | tf_op jit(solution)/shard_map/all_gather | solution.py:25
  196.6 48.9 %collective-permute-start = (f32[4096,128]{1,0:T(8,128)}, f32[4096,128]{1,0:T(8,128)S(1)}, u32[]{:S(2)}, u32[]{:S(2)}) collective-permute-start(f32[4096,128]{1,0:T(8,128)} %get-tuple-element.6), channel_id=1, source_target_pairs={{0,8},{8,16},{16,24},{1,9},{9,17},{17,25},{2,10},{10,18},{18,26},{... | collective-permute-start | bytes 6291464 | tf_op jit(solution)/shard_map/ppermute | solution.py:12
  245.5 1.3 copy-start.3
  246.9 3.4 copy-start
  290.9 60.5 %all-gather.19.cloned.1.call-start = ((), (), s32[]{:S(2)}) async-start(), calls=%async_computation.3 | async-start | bytes 2359296 | tf_op jit(solution)/shard_map/all_gather | solution.py:30
  322.2 88.4 %all-gather.21.cloned.1.call-start = ((), (), s32[]{:S(2)}) async-start(), calls=%async_computation.4 | async-start | bytes 2359296 | tf_op jit(solution)/shard_map/all_gather | solution.py:36
  361.6 117.8 %all-gather.29.cloned.1.call-start = ((), (), s32[]{:S(2)}) async-start(), calls=%async_computation.8 | async-start | bytes 1310720 | tf_op jit(solution)/shard_map/all_gather | solution.py:25
  361.6 49.0 %collective-permute-start.1 = (f32[4096,128]{1,0:T(8,128)}, f32[4096,128]{1,0:T(8,128)}, u32[]{:S(2)}, u32[]{:S(2)}) collective-permute-start(f32[4096,128]{1,0:T(8,128)} %get-tuple-element.5), channel_id=1, source_target_pairs={{0,8},{8,16},{16,24},{1,9},{9,17},{17,25},{2,10},{10,18},{18,26},{... | collective-permute-start | bytes 6291464 | tf_op jit(solution)/shard_map/ppermute | solution.py:12
  412.4 40.3 %copy-start.4 = (f32[1,512,128]{2,1,0:T(8,128)S(1)}, f32[1,512,128]{2,1,0:T(8,128)}, u32[]{:S(2)}) copy-start(f32[1,512,128]{2,1,0:T(8,128)} %get-tuple-element.7) | copy-start | bytes 786436
  452.3 59.7 %all-gather.23.cloned.1.call-start = ((), (), s32[]{:S(2)}) async-start(), calls=%async_computation.5 | async-start | bytes 2359296 | tf_op jit(solution)/shard_map/all_gather | solution.py:30
  481.3 40.1 %copy-start.1 = (f32[128,512]{0,1:T(8,128)S(1)}, f32[128,512]{0,1:T(8,128)}, u32[]{:S(2)}) copy-start(f32[128,512]{0,1:T(8,128)} %fusion.18) | copy-start | bytes 786436
  481.4 40.1 %copy-start.2 = (f32[128,512]{0,1:T(8,128)S(1)}, f32[128,512]{0,1:T(8,128)}, u32[]{:S(2)}) copy-start(f32[128,512]{0,1:T(8,128)} %fusion.19) | copy-start | bytes 786436
Sparse Core Ops, SparseCore 0:
  8.9 84.7 all-gather.12
  125.6 24.9 all-gather.24
  152.8 29.1 all-gather.14
  192.2 28.5 all-gather.16
  291.1 26.7 all-gather.26
  322.3 29.1 all-gather.18
  361.7 28.5 all-gather.20
  452.5 26.8 all-gather.28
  482.9 29.1 all-gather.22
